TPU v7x, 32 devices: a whole 2x2x4 slice. The times are simulated.
32 devices in a mesh: freq: 2 (over x), clus: 8 (over z, y), rhs: 2 (over core).
Axes of the slice: x: 2, y: 2, z: 4, core: 2. Of those that a mesh axis runs over, the one named last changes fastest.
Arguments:
- input_columns: bfloat16 [256, 2, 128, 128], P(('freq', 'clus'), None, 'rhs'), parts along dimension 0, may hold values from -6 to 6
- near_blocks: bfloat16 [256, 7, 2, 128, 128], P(('freq', 'clus')), parts along dimension 0, may hold values from -0.125 to 0.125
- near_off: int32 [128, 7], P('clus'), may hold values from -16 to 16, as said below
- basis_in: bfloat16 [256, 2, 128, 64], P(('freq', 'clus')), parts along dimension 0, may hold values from -0.375 to 0.375
- coupling: bfloat16 [16, 8, 4, 2, 64, 64], P(('freq', 'clus')), parts along dimension 0, may hold values from -0.375 to 0.375
- basis_out: bfloat16 [256, 2, 64, 128], P(('freq', 'clus')), parts along dimension 0, may hold values from -0.5 to 0.5
- far_pairs: int32 [8, 8, 4, 2], replicated, may hold values from 0 to 15
- far_rank: int32 [8, 8, 4], replicated, may hold values from 0 to 64, as said below
Outputs:
- first_image: bfloat16 [256, 2, 128, 128], P(('freq', 'clus'), None, 'rhs'), parts along dimension 0
- second_image: bfloat16 [256, 2, 128, 128], P(('freq', 'clus'), None, 'rhs'), parts along dimension 0
There are 2 independent parts, one for each index of `freq`. A program takes and returns all parts, laid end to end along the dimension named above; an argument that names none is the same for every part. Nothing has to cross between parts.
Inputs may be any that keep to these rules, and one draw needn't show every extreme that they name: `near_off`: each row holds 7 distinct offsets, the first of them 0. `far_rank`: a rank of 0 marks an empty slot.
All inputs are finite; a program needn't handle non-finite values.
Results may differ from a plain program's by a relative error of at most 0.0056.
Values may be sent and summed in bfloat16 or wider, within the bound.
A program may use at most 128 MiB of HBM per device.

v0:
```python
import jax
import jax.numpy as jnp
from jax import lax
from jax.sharding import PartitionSpec as P


def padded_2(block, sides, width):
    for axis, dim in sides:
        count = lax.axis_size(axis)
        forward = [(i, i + 1) for i in range(count - 1)]
        backward = [(target, source) for source, target in forward]
        low = lax.ppermute(
            lax.slice_in_dim(block, block.shape[dim] - width, None, axis=dim), axis, forward
        )
        high = lax.ppermute(lax.slice_in_dim(block, 0, width, axis=dim), axis, backward)
        block = jnp.concatenate([low, block, high], axis=dim)
    return block


def basis_inward(basis):
    real_part = basis[:, 0]
    imag_part = basis[:, 1]
    upper = jnp.concatenate([real_part, imag_part], -1)
    lower = jnp.concatenate([-imag_part, real_part], -1)
    return jnp.stack([upper, lower], 1)


def basis_outward(basis):
    real_part = basis[:, 0]
    imag_part = basis[:, 1]
    upper = jnp.stack([real_part, imag_part], 2)
    lower = jnp.stack([-imag_part, real_part], 2)
    return jnp.concatenate([upper, lower], 1)


def coupling_square(coupling):
    real_part = coupling[..., 0, :, :]
    imag_part = coupling[..., 1, :, :]
    upper = jnp.concatenate([real_part, imag_part], -1)
    lower = jnp.concatenate([-imag_part, real_part], -1)
    return jnp.concatenate([upper, lower], -2)


def transposed_apply(
    columns, near_blocks, near_off, wide_in, square, wide_out, sending, incoming, incoming_rank
):
    clusters_here = columns.shape[0]
    padded = padded_2(columns, (("clus", 0),), clusters_here)
    row_index = jnp.arange(clusters_here, dtype=jnp.int32)[:, None] + near_off + clusters_here
    gathered = padded[row_index]
    products = jnp.einsum(
        "cjprt,cjqts->cpqrs", gathered, near_blocks, preferred_element_type=jnp.float32
    )
    near_real = products[:, 0, 0] - products[:, 1, 1]
    near_imag = products[:, 0, 1] + products[:, 1, 0]
    coeffs = jnp.einsum(
        "cprt,cptk->crk", columns, wide_in, preferred_element_type=jnp.float32
    ).astype(jnp.bfloat16)
    outgoing = coeffs[sending[..., 0]]
    received = lax.all_to_all(outgoing, "clus", split_axis=0, concat_axis=0, tiled=True)
    double_rank = coeffs.shape[-1]
    rank_mask = (
        jnp.arange(double_rank, dtype=jnp.int32) % (double_rank // 2) < incoming_rank[..., None]
    )
    masked = received * rank_mask[:, :, None, :].astype(jnp.bfloat16)
    weighted = jnp.einsum("ejrk,ejkl->ejrl", masked, square, preferred_element_type=jnp.float32)
    weighted = weighted * rank_mask[:, :, None, :].astype(jnp.float32)
    slot_count = weighted.shape[0] * weighted.shape[1]
    one_hot = (
        incoming[..., 1].reshape(-1)[None, :] == jnp.arange(clusters_here, dtype=jnp.int32)[:, None]
    ).astype(jnp.float32)
    summed = jnp.dot(one_hot, weighted.reshape(slot_count, -1), precision=lax.Precision.HIGHEST)
    summed = summed.reshape(clusters_here, weighted.shape[2], double_rank).astype(jnp.bfloat16)
    far_term = jnp.einsum("crk,ckqs->cqrs", summed, wide_out, preferred_element_type=jnp.float32)
    return (jnp.stack([near_real, near_imag], 1) + far_term).astype(jnp.bfloat16)


def on_device(
    input_columns, near_blocks, near_off, basis_in, coupling, basis_out, far_pairs, far_rank
):
    position = lax.axis_index("clus")
    sending = lax.dynamic_index_in_dim(far_pairs, position, 0, keepdims=False)
    incoming = lax.dynamic_index_in_dim(far_pairs, position, 1, keepdims=False)
    incoming_rank = lax.dynamic_index_in_dim(far_rank, position, 1, keepdims=False)
    wide_in = basis_inward(basis_in)
    wide_out = basis_outward(basis_out)
    square = coupling_square(coupling[0])
    images = []
    current = input_columns
    for sweep_index in range(2):
        current = transposed_apply(
            current,
            near_blocks,
            near_off,
            wide_in,
            square,
            wide_out,
            sending,
            incoming,
            incoming_rank,
        )
        images.append(current)
    return (images[0], images[1])


def solution(mesh):
    in_specs = (
        P(("freq", "clus"), None, "rhs", None),
        P(("freq", "clus"), None, None, None, None),
        P("clus", None),
        P(("freq", "clus"), None, None, None),
        P(("freq", "clus"), None, None, None, None, None),
        P(("freq", "clus"), None, None, None),
        P(),
        P(),
    )
    out_specs = (P(("freq", "clus"), None, "rhs", None), P(("freq", "clus"), None, "rhs", None))
    return jax.shard_map(
        on_device, mesh=mesh, in_specs=in_specs, out_specs=out_specs, check_vma=False
    )
```

profile of v0, /device:TPU:8, one launch (start us, length us, event | category | flops | bytes accessed | tf_op | source)
XLA Modules:
  0.0 94.2 jit_solution(17048337473833803547)
XLA Ops:
  0.6 3.4 %collective-permute-start = (bf16[16,2,64,128]{3,2,1,0:T(8,128)(2,1)}, bf16[16,2,64,128]{3,2,1,0:T(8,128)(2,1)}, u32[]{:S(2)}, u32[]{:S(2)}) collective-permute-start(bf16[16,2,64,128]{3,2,1,0:T(8,128)(2,1)} %param.8), channel_id=1, source_target_pairs={{0,2},{2,4},{4,6},{6,8},{8,10},{10,12},{12,14},{1,3},{3,5},{5,7},{... | collective-permute-start | bytes 1572872 | tf_op jit(solution)/shard_map/ppermute | solution.py:12
  4.1 3.3 %collective-permute-start.1 = (bf16[16,2,64,128]{3,2,1,0:T(8,128)(2,1)}, bf16[16,2,64,128]{3,2,1,0:T(8,128)(2,1)}, u32[]{:S(2)}, u32[]{:S(2)}) collective-permute-start(bf16[16,2,64,128]{3,2,1,0:T(8,128)(2,1)} %param.8), channel_id=1, source_target_pairs={{2,0},{4,2},{6,4},{8,6},{10,8},{12,10},{14,12},{3,1},{5,3},{7,5},{... | collective-permute-start | bytes 1572872 | tf_op jit(solution)/shard_map/ppermute | solution.py:15
  7.4 1.1 %fusion.53 = (bf16[16,1,128,64]{2,3,1,0:T(8,128)(2,1)S(1)}, bf16[16,1,128,64]{2,3,1,0:T(8,128)(2,1)S(1)}) fusion(bf16[16,2,128,64]{2,3,1,0:T(8,128)(2,1)} %param.11), kind=kLoop, calls=%fused_computation.86 | loop fusion | bytes 1048576 | tf_op jit(solution)/shard_map/slice | solution.py:22
  8.5 0.3 copy.89
  8.9 0.3 copy.88
  9.2 0.1 copy.49
  9.4 0.6 maximum_bitcast_fusion
  10.0 0.3 fusion.22
  10.4 1.4 %gather_fusion.1 = bf16[32,64,128]{2,1,0:T(8,128)(2,1)} fusion(bf16[16,64,128]{2,1,0:T(8,128)(2,1)S(1)} %fusion.22, s32[1024]{0:T(1024)S(1)} %pad_clamp_fusion), kind=kCustom, calls=%fused_computation.1 | custom fusion | bytes 1048704 | tf_op jit(solution)/shard_map/gather | solution.py:59
  11.8 6.2 %all-to-all-start = ((bf16[8,4,64,128]{3,2,1,0:T(8,128)(2,1)}), bf16[8,4,64,128]{3,2,1,0:T(8,128)(2,1)}, u32[]{:S(2)}, u32[]{:S(2)}) async-start(bf16[8,4,64,128]{3,2,1,0:T(8,128)(2,1)} %bitcast.22), calls=%async_computation | async-start | bytes 1048576 | tf_op jit(solution)/shard_map/all_to_all | solution.py:60
  17.9 0.1 constant_dynamic-slice_fusion.2
  18.1 0.9 slice_bitcast_fusion.6
  19.0 0.1 copy.50
  19.1 0.1 copy.51
  19.2 0.1 copy.36
  19.3 0.1 reshape.117
  19.5 0.1 copy.144
  19.6 0.1 copy.43
  19.8 0.1 copy.44
  20.0 1.2 %slice_bitcast_fusion.2 = (bf16[8,4,64,64]{3,2,1,0:T(8,128)(2,1)}, bf16[8,4,64,64]{3,2,1,0:T(8,128)(2,1)}) fusion(bf16[8,4,2,64,64]{4,3,1,0,2:T(8,128)(2,1)S(1)} %bitcast.157), kind=kLoop, calls=%fused_computation.48 | loop fusion | bytes 1048576 | tf_op jit(solution)/shard_map/squeeze | solution.py:38
  21.2 10.5 %collective-permute-done = bf16[16,2,64,128]{3,2,1,0:T(8,128)(2,1)} collective-permute-done((bf16[16,2,64,128]{3,2,1,0:T(8,128)(2,1)}, bf16[16,2,64,128]{3,2,1,0:T(8,128)(2,1)}, u32[]{:S(2)}, u32[]{:S(2)}) %collective-permute-start) | collective-permute-done | bytes 524320 | tf_op jit(solution)/shard_map/ppermute | solution.py:12
  31.7 1.3 %collective-permute-done.1 = bf16[16,2,64,128]{3,2,1,0:T(8,128)(2,1)} collective-permute-done((bf16[16,2,64,128]{3,2,1,0:T(8,128)(2,1)}, bf16[16,2,64,128]{3,2,1,0:T(8,128)(2,1)}, u32[]{:S(2)}, u32[]{:S(2)}) %collective-permute-start.1) | collective-permute-done | bytes 524320 | tf_op jit(solution)/shard_map/ppermute | solution.py:15
  33.0 1.5 %pad_maximum_fusion = bf16[48,2,64,128]{3,2,1,0:T(8,128)(2,1)S(1)} fusion(bf16[16,2,64,128]{3,2,1,0:T(8,128)(2,1)} %collective-permute-done.1, bf16[16,2,64,128]{3,2,1,0:T(8,128)(2,1)} %param.8, bf16[16,2,64,128]{3,2,1,0:T(8,128)(2,1)} %collective-permute-done), kind=kLoop, calls=%fused_computation.12 | loop fusion | flops 1572864 | bytes 3145728 | tf_op jit(solution)/shard_map/concatenate | solution.py:16
  34.5 2.9 %gather_fusion = bf16[112,2,64,128]{3,2,1,0:T(8,128)(2,1)} fusion(bf16[48,2,64,128]{3,2,1,0:T(8,128)(2,1)S(1)} %pad_maximum_fusion, s32[1024]{0:T(1024)S(1)} %pad_clamp_fusion.1), kind=kCustom, calls=%fused_computation | custom fusion | bytes 7340480 | tf_op jit(solution)/shard_map/gather | solution.py:50
  37.3 5.7 %fusion.6 = f32[16,2,2,64,128]{4,3,2,1,0:T(8,128)S(1)} fusion(bf16[16,7,2,64,128,1]{4,3,2,1,0,5:T(8,128)(2,1)} %bitcast.160, bf16[16,7,2,128,128]{4,3,2,1,0:T(8,128)(2,1)} %param.9), kind=kOutput, calls=%fused_computation.10 | convolution fusion | flops 939524096 | bytes 13107200 | tf_op jit(solution)/shard_map/cjprt,cjqts->cpqrs/dot_general | solution.py:51
  43.2 0.9 copy-done.6
  44.1 2.1 %convolution_multiply_fusion.1 = f32[8,4,64,128]{3,2,1,0:T(8,128)S(1)} fusion(f32[8,4,128]{2,1,0:T(4,128)S(1)} %get-tuple-element.15, bf16[8,4,64,128]{3,2,1,0:T(8,128)(2,1)} %all-to-all-done, bf16[8,4,128]{2,1,0:T(4,128)(2,1)S(1)} %get-tuple-element.14, bf16[8,4,64,64]{3,2,1,0:T(8,128)(2,1)} %get-tuple-element.7, bf16[8,4,64,64]{3,2,1,0:T(8,128)(2,1)S(1)} %fusion.52, ...), kind=kOutput, calls=%fused_computation.17 | convolution fusion | flops 71827456 | bytes 2383872 | tf_op jit(solution)/shard_map/ejrk,ejkl->ejrl/dot_general | solution.py:66
  46.3 1.1 %fusion.26 = bf16[16,64,128]{2,0,1:T(8,128)(2,1)S(1)} fusion(s32[32]{0:T(128)S(1)} %eq.11, f32[4,8,64,128]{3,2,1,0:T(8,128)S(1)} %bitcast.163), kind=kOutput, calls=%fused_computation.32 | convolution fusion | flops 50332160 | bytes 1310848 | tf_op jit(solution)/shard_map/dot_general | solution.py:72
  47.4 0.3 fusion.19
  47.7 3.1 %collective-permute-start.2 = (bf16[16,2,64,128]{3,2,0,1:T(8,128)(2,1)S(1)}, bf16[16,2,64,128]{3,2,0,1:T(8,128)(2,1)S(1)}, u32[]{:S(2)}, u32[]{:S(2)}) collective-permute-start(bf16[16,2,64,128]{3,2,0,1:T(8,128)(2,1)S(1)} %fusion.19), channel_id=1, source_target_pairs={{0,2},{2,4},{4,6},{6,8},{8,10},{10,12},{12,14},{1,3},{3,5},{5,7},{... | collective-permute-start | bytes 1572872 | tf_op jit(solution)/shard_map/ppermute | solution.py:12
  50.8 3.6 %collective-permute-start.3 = (bf16[16,2,64,128]{3,2,0,1:T(8,128)(2,1)S(1)}, bf16[16,2,64,128]{3,2,0,1:T(8,128)(2,1)}, u32[]{:S(2)}, u32[]{:S(2)}) collective-permute-start(bf16[16,2,64,128]{3,2,0,1:T(8,128)(2,1)S(1)} %fusion.19), channel_id=1, source_target_pairs={{2,0},{4,2},{6,4},{8,6},{10,8},{12,10},{14,12},{3,1},{5,3},{7,5},{... | collective-permute-start | bytes 1572872 | tf_op jit(solution)/shard_map/ppermute | solution.py:15
  54.5 0.8 copy.60
  55.3 0.3 fusion.20
  55.6 1.4 %gather_fusion.3 = bf16[32,64,128]{2,1,0:T(8,128)(2,1)} fusion(bf16[16,64,128]{2,1,0:T(8,128)(2,1)S(1)} %fusion.20, s32[1024]{0:T(1024)S(1)} %pad_clamp_fusion), kind=kCustom, calls=%fused_computation.3 | custom fusion | bytes 1048704 | tf_op jit(solution)/shard_map/gather | solution.py:59
  57.1 5.3 %all-to-all-start.1 = ((bf16[8,4,64,128]{3,2,1,0:T(8,128)(2,1)}), bf16[8,4,64,128]{3,2,1,0:T(8,128)(2,1)S(1)}, u32[]{:S(2)}, u32[]{:S(2)}) async-start(bf16[8,4,64,128]{3,2,1,0:T(8,128)(2,1)} %bitcast.40), calls=%async_computation.1 | async-start | bytes 1048576 | tf_op jit(solution)/shard_map/all_to_all | solution.py:60
  62.4 14.2 %collective-permute-done.2 = bf16[16,2,64,128]{3,2,0,1:T(8,128)(2,1)S(1)} collective-permute-done((bf16[16,2,64,128]{3,2,0,1:T(8,128)(2,1)S(1)}, bf16[16,2,64,128]{3,2,0,1:T(8,128)(2,1)S(1)}, u32[]{:S(2)}, u32[]{:S(2)}) %collective-permute-start.2) | collective-permute-done | bytes 524320 | tf_op jit(solution)/shard_map/ppermute | solution.py:12
  76.6 0.8 copy-done.9
  77.4 2.5 %collective-permute-done.3 = bf16[16,2,64,128]{3,2,0,1:T(8,128)(2,1)} collective-permute-done((bf16[16,2,64,128]{3,2,0,1:T(8,128)(2,1)S(1)}, bf16[16,2,64,128]{3,2,0,1:T(8,128)(2,1)}, u32[]{:S(2)}, u32[]{:S(2)}) %collective-permute-start.3) | collective-permute-done | bytes 524320 | tf_op jit(solution)/shard_map/ppermute | solution.py:15
  79.9 1.4 %pad_maximum_fusion.1 = bf16[48,2,64,128]{3,2,0,1:T(8,128)(2,1)S(1)} fusion(bf16[16,2,64,128]{3,2,0,1:T(8,128)(2,1)} %collective-permute-done.3, bf16[16,2,64,128]{3,2,0,1:T(8,128)(2,1)S(1)} %fusion.19, bf16[16,2,64,128]{3,2,0,1:T(8,128)(2,1)} %copy-done.9), kind=kLoop, calls=%fused_computation.13 | loop fusion | flops 1572864 | bytes 3145728 | tf_op jit(solution)/shard_map/concatenate | solution.py:16
  81.3 2.9 %gather_fusion.2 = bf16[112,2,64,128]{3,2,1,0:T(8,128)(2,1)} fusion(bf16[48,2,64,128]{3,2,0,1:T(8,128)(2,1)S(1)} %pad_maximum_fusion.1, s32[1024]{0:T(1024)S(1)} %pad_clamp_fusion.1), kind=kCustom, calls=%fused_computation.2 | custom fusion | bytes 7340480 | tf_op jit(solution)/shard_map/gather | solution.py:50
  84.1 5.7 %fusion.11 = f32[16,2,2,64,128]{4,3,2,1,0:T(8,128)S(1)} fusion(bf16[16,7,2,64,128,1]{4,3,2,1,0,5:T(8,128)(2,1)} %bitcast.159, bf16[16,7,2,128,128]{4,3,2,1,0:T(8,128)(2,1)} %param.9), kind=kOutput, calls=%fused_computation.11 | convolution fusion | flops 939524096 | bytes 13107200 | tf_op jit(solution)/shard_map/cjprt,cjqts->cpqrs/dot_general | solution.py:51
  90.0 0.9 copy-done.4
  90.9 0.2 copy-done.7
  91.1 0.2 copy-done.8
  91.2 0.7 convolution_multiply_fusion
  92.0 1.1 %fusion.23 = bf16[16,64,128]{2,0,1:T(8,128)(2,1)S(1)} fusion(s32[32]{0:T(128)S(1)} %eq.11, f32[4,8,64,128]{3,2,1,0:T(8,128)S(1)} %bitcast.162), kind=kOutput, calls=%fused_computation.29 | convolution fusion | flops 50332160 | bytes 1310848 | tf_op jit(solution)/shard_map/dot_general | solution.py:72
  93.1 0.3 fusion.18
  93.4 0.8 copy.61
  (48 shorter events, 0.8 us)
Async XLA Ops:
  0.6 8.5 %copy-start = (s32[8,8,4,2]{1,3,2,0:T(2,128)S(1)}, s32[8,8,4,2]{1,3,2,0:T(2,128)}, u32[]{:S(2)}) copy-start(s32[8,8,4,2]{1,3,2,0:T(2,128)} %param.14) | copy-start | bytes 6148
  0.6 31.1 %collective-permute-start = (bf16[16,2,64,128]{3,2,1,0:T(8,128)(2,1)}, bf16[16,2,64,128]{3,2,1,0:T(8,128)(2,1)}, u32[]{:S(2)}, u32[]{:S(2)}) collective-permute-start(bf16[16,2,64,128]{3,2,1,0:T(8,128)(2,1)} %param.8), channel_id=1, source_target_pairs={{0,2},{2,4},{4,6},{6,8},{8,10},{10,12},{12,14},{1,3},{3,5},{5,7},{... | collective-permute-start | bytes 1572872 | tf_op jit(solution)/shard_map/ppermute | solution.py:12
  4.1 28.9 %collective-permute-start.1 = (bf16[16,2,64,128]{3,2,1,0:T(8,128)(2,1)}, bf16[16,2,64,128]{3,2,1,0:T(8,128)(2,1)}, u32[]{:S(2)}, u32[]{:S(2)}) collective-permute-start(bf16[16,2,64,128]{3,2,1,0:T(8,128)(2,1)} %param.8), channel_id=1, source_target_pairs={{2,0},{4,2},{6,4},{8,6},{10,8},{12,10},{14,12},{3,1},{5,3},{7,5},{... | collective-permute-start | bytes 1572872 | tf_op jit(solution)/shard_map/ppermute | solution.py:15
  8.8 1.2 %copy-start.5 = (bf16[16,2,64,128]{3,2,1,0:T(8,128)(2,1)S(1)}, bf16[16,2,64,128]{3,2,1,0:T(8,128)(2,1)}, u32[]{:S(2)}) copy-start(bf16[16,2,64,128]{3,2,1,0:T(8,128)(2,1)} %param.8) | copy-start | bytes 1572868
  10.0 8.1 %copy-start.1 = (bf16[16,2,64,128]{3,2,1,0:T(8,128)(2,1)S(1)}, bf16[16,2,64,128]{3,2,1,0:T(8,128)(2,1)}, u32[]{:S(2)}) copy-start(bf16[16,2,64,128]{3,2,1,0:T(8,128)(2,1)} %param.13) | copy-start | bytes 1572868
  10.3 8.6 %copy-start.14 = (s32[8,8,4]{1,2,0:T(4,128)S(1)}, s32[8,8,4]{1,2,0:T(4,128)}, u32[]{:S(2)}) copy-start(s32[8,8,4]{1,2,0:T(4,128)} %param.15) | copy-start | bytes 3076
  10.3 8.9 %copy-start.15 = (s32[16,7]{0,1:T(8,128)S(1)}, s32[16,7]{0,1:T(8,128)}, u32[]{:S(2)}) copy-start(s32[16,7]{0,1:T(8,128)} %param.10) | copy-start | bytes 1348
  10.3 9.2 %copy-start.2 = (bf16[1,8,4,2,64,64]{5,4,3,2,1,0:T(8,128)(2,1)S(1)}, bf16[1,8,4,2,64,64]{5,4,3,2,1,0:T(8,128)(2,1)}, u32[]{:S(2)}) copy-start(bf16[1,8,4,2,64,64]{5,4,3,2,1,0:T(8,128)(2,1)} %param.12) | copy-start | bytes 1572868
  11.8 31.5 %all-to-all-start = ((bf16[8,4,64,128]{3,2,1,0:T(8,128)(2,1)}), bf16[8,4,64,128]{3,2,1,0:T(8,128)(2,1)}, u32[]{:S(2)}, u32[]{:S(2)}) async-start(bf16[8,4,64,128]{3,2,1,0:T(8,128)(2,1)} %bitcast.22), calls=%async_computation | async-start | bytes 1048576 | tf_op jit(solution)/shard_map/all_to_all | solution.py:60
  20.0 23.2 %copy-start.3 = (bf16[8,4,64,64]{3,2,1,0:T(8,128)(2,1)}, bf16[8,4,64,64]{3,2,1,0:T(8,128)(2,1)S(1)}, u32[]{:S(2)}) copy-start(bf16[8,4,64,64]{3,2,1,0:T(8,128)(2,1)S(1)} %fusion.52) | copy-start | bytes 786436
  43.1 1.0 %copy-start.6 = (bf16[8,4,64,64]{3,2,1,0:T(8,128)(2,1)S(1)}, bf16[8,4,64,64]{3,2,1,0:T(8,128)(2,1)}, u32[]{:S(2)}) copy-start(bf16[8,4,64,64]{3,2,1,0:T(8,128)(2,1)} %get-tuple-element.6) | copy-start | bytes 786436
  44.1 3.2 %copy-start.10 = (bf16[16,64,1,128]{3,1,2,0:T(8,128)(2,1)S(1)}, bf16[16,64,1,128]{3,1,2,0:T(8,128)(2,1)}, u32[]{:S(2)}) copy-start(bf16[16,64,1,128]{3,1,2,0:T(8,128)(2,1)} %get-tuple-element.12) | copy-start | bytes 786436
  44.1 3.2 %copy-start.12 = (bf16[16,64,1,128]{3,1,2,0:T(8,128)(2,1)S(1)}, bf16[16,64,1,128]{3,1,2,0:T(8,128)(2,1)}, u32[]{:S(2)}) copy-start(bf16[16,64,1,128]{3,1,2,0:T(8,128)(2,1)} %get-tuple-element.13) | copy-start | bytes 786436
  47.7 28.9 %collective-permute-start.2 = (bf16[16,2,64,128]{3,2,0,1:T(8,128)(2,1)S(1)}, bf16[16,2,64,128]{3,2,0,1:T(8,128)(2,1)S(1)}, u32[]{:S(2)}, u32[]{:S(2)}) collective-permute-start(bf16[16,2,64,128]{3,2,0,1:T(8,128)(2,1)S(1)} %fusion.19), channel_id=1, source_target_pairs={{0,2},{2,4},{4,6},{6,8},{8,10},{10,12},{12,14},{1,3},{3,5},{5,7},{... | collective-permute-start | bytes 1572872 | tf_op jit(solution)/shard_map/ppermute | solution.py:12
  50.8 29.0 %collective-permute-start.3 = (bf16[16,2,64,128]{3,2,0,1:T(8,128)(2,1)S(1)}, bf16[16,2,64,128]{3,2,0,1:T(8,128)(2,1)}, u32[]{:S(2)}, u32[]{:S(2)}) collective-permute-start(bf16[16,2,64,128]{3,2,0,1:T(8,128)(2,1)S(1)} %fusion.19), channel_id=1, source_target_pairs={{2,0},{4,2},{6,4},{8,6},{10,8},{12,10},{14,12},{3,1},{5,3},{7,5},{... | collective-permute-start | bytes 1572872 | tf_op jit(solution)/shard_map/ppermute | solution.py:15
  57.1 33.0 %all-to-all-start.1 = ((bf16[8,4,64,128]{3,2,1,0:T(8,128)(2,1)}), bf16[8,4,64,128]{3,2,1,0:T(8,128)(2,1)S(1)}, u32[]{:S(2)}, u32[]{:S(2)}) async-start(bf16[8,4,64,128]{3,2,1,0:T(8,128)(2,1)} %bitcast.40), calls=%async_computation.1 | async-start | bytes 1048576 | tf_op jit(solution)/shard_map/all_to_all | solution.py:60
  76.6 0.8 copy-start.9
  89.9 1.0 %copy-start.4 = (bf16[8,4,64,64]{3,2,1,0:T(8,128)(2,1)S(1)}, bf16[8,4,64,64]{3,2,1,0:T(8,128)(2,1)}, u32[]{:S(2)}) copy-start(bf16[8,4,64,64]{3,2,1,0:T(8,128)(2,1)} %copy-done.3) | copy-start | bytes 786436
  89.9 1.2 %copy-start.7 = (bf16[8,4,64,64]{3,2,1,0:T(8,128)(2,1)S(1)}, bf16[8,4,64,64]{3,2,1,0:T(8,128)(2,1)}, u32[]{:S(2)}) copy-start(bf16[8,4,64,64]{3,2,1,0:T(8,128)(2,1)} %get-tuple-element.6) | copy-start | bytes 786436
  89.9 1.3 %copy-start.8 = (bf16[8,4,64,64]{3,2,1,0:T(8,128)(2,1)S(1)}, bf16[8,4,64,64]{3,2,1,0:T(8,128)(2,1)}, u32[]{:S(2)}) copy-start(bf16[8,4,64,64]{3,2,1,0:T(8,128)(2,1)} %get-tuple-element.7) | copy-start | bytes 786436
  91.2 1.8 %copy-start.11 = (bf16[16,64,1,128]{3,1,2,0:T(8,128)(2,1)S(1)}, bf16[16,64,1,128]{3,1,2,0:T(8,128)(2,1)}, u32[]{:S(2)}) copy-start(bf16[16,64,1,128]{3,1,2,0:T(8,128)(2,1)} %get-tuple-element.12) | copy-start | bytes 786436
  91.2 1.8 %copy-start.13 = (bf16[16,64,1,128]{3,1,2,0:T(8,128)(2,1)S(1)}, bf16[16,64,1,128]{3,1,2,0:T(8,128)(2,1)}, u32[]{:S(2)}) copy-start(bf16[16,64,1,128]{3,1,2,0:T(8,128)(2,1)} %get-tuple-element.13) | copy-start | bytes 786436
where the time goes:
time: 94.9 us; the launch traced here: 94.2 us
  waiting for transfers between devices  28.5 us (30%)
  starting transfers between devices  25 us (26%)
  local copies, waits for them, and re-layouts  17.9 us (19%)
  matrix products  17.7 us (19%)
  other arithmetic  4 us (4%)
  between operations  1.07 us (1%)
    ppermute x2, waiting for transfers between devices, padded_2(): lax.ppermute(lax.slice_in_dim(block, block.shape[dim] - width, None, axis...  24.7 us
    all_to_all x2, starting transfers between devices, transposed_apply(): lax.all_to_all(outgoing, 'clus', split_axis=0, concat_axis=0, tiled=True)  11.5 us
    dot_general x2, matrix products, transposed_apply(): jnp.einsum('cjprt,cjqts->cpqrs', gathered, near_blocks, preferred_element...  11.5 us
    ppermute x2, starting transfers between devices, padded_2(): lax.ppermute(lax.slice_in_dim(block, 0, width, axis=dim), axis, backward)  6.92 us
    ppermute x2, starting transfers between devices, padded_2(): lax.ppermute(lax.slice_in_dim(block, block.shape[dim] - width, None, axis...  6.57 us
    gather x2, local copies, waits for them, and re-layouts, transposed_apply(): gathered = padded[row_index]  5.71 us
    unnamed x37, local copies, waits for them, and re-layouts  5.26 us
    ppermute x2, waiting for transfers between devices, padded_2(): lax.ppermute(lax.slice_in_dim(block, 0, width, axis=dim), axis, backward)  3.74 us
  transfers between devices with their start and end apart: 6, of which 4 were waited for; matrix products, arithmetic and copies ran while one was open for 32% of the time, Pallas kernels for 0%

commit v1 on v0

v1 whole, which is shorter than its diff:
```python
import functools

import jax
import jax.numpy as jnp
from jax import lax
from jax.experimental import pallas as pl
from jax.experimental.pallas import tpu as pltpu
from jax.sharding import PartitionSpec as P

F32 = jnp.float32
BF16 = jnp.bfloat16

HI_A, HI_B, LO_A, LO_B = range(4)


def complex_rows(product):
    half_rows, half_cols = product.shape[0] // 2, product.shape[1] // 2
    real = product[:half_rows, :half_cols] - product[half_rows:, half_cols:]
    imag = product[:half_rows, half_cols:] + product[half_rows:, :half_cols]
    return real, imag


def kernel(
    n, off, pairs, rank, columns, near_hbm, basis_in, coupling, basis_out,
    first, second,
    near, own_0, own_1, image, hi_a_0, hi_b_0, lo_a_0, lo_b_0, hi_a_1, hi_b_1, lo_a_1, lo_b_1, total, coeffs, outgoing, received, square, weighted,
    near_sem, halo_send, halo_recv, slot_send, slot_recv,
):
    me = lax.axis_index("clus")
    clusters, rows, leaf = columns.shape
    half = clusters // 2
    slots = coupling.shape[1]
    width = coupling.shape[3]
    near_per = near.shape[1]
    rhs = rows // 2

    def fetch():
        return pltpu.make_async_copy(near_hbm, near, near_sem)

    fetch().start()
    barrier = pltpu.get_barrier_semaphore()

    @pl.loop(1, n)
    def _(k):
        pl.semaphore_signal(barrier, inc=1, device_id={"clus": lax.rem(me + k, n)})

    own = (own_0, own_1)
    buffers = ((hi_a_0, hi_b_0, lo_a_0, lo_b_0), (hi_a_1, hi_b_1, lo_a_1, lo_b_1))
    zero = jnp.zeros((rows, leaf), BF16)
    for sweep in range(2):
        own[sweep][clusters] = zero
        for buffer in buffers[sweep]:
            buffer[half] = zero

    @pl.when(me == 0)
    def _():
        for sweep in range(2):
            for chunk in (LO_A, LO_B):
                buffers[sweep][chunk][...] = jnp.zeros_like(buffers[sweep][chunk])

    @pl.when(me == n - 1)
    def _():
        for sweep in range(2):
            for chunk in (HI_A, HI_B):
                buffers[sweep][chunk][...] = jnp.zeros_like(buffers[sweep][chunk])

    pl.semaphore_wait(barrier, n - 1)

    starts = (0, half, half, 0)

    def halo(sweep, chunk):
        to_left = chunk in (HI_A, HI_B)
        source = columns if sweep == 0 else image
        peer = lax.rem(me + (n - 1 if to_left else 1), n)
        return pltpu.make_async_remote_copy(
            src_ref=source.at[pl.ds(starts[chunk], half)],
            dst_ref=buffers[sweep][chunk].at[pl.ds(0, half)],
            send_sem=halo_send.at[sweep, chunk],
            recv_sem=halo_recv.at[sweep, chunk],
            device_id={"clus": peer},
        )

    def send_halo(sweep, chunk):
        @pl.when(me > 0 if chunk in (HI_A, HI_B) else me < n - 1)
        def _():
            halo(sweep, chunk).start()

    def halo_sent(sweep, chunk):
        @pl.when(me > 0 if chunk in (HI_A, HI_B) else me < n - 1)
        def _():
            halo(sweep, chunk).wait_send()

    def wait_halo(sweep, chunk):
        @pl.when(me < n - 1 if chunk in (HI_A, HI_B) else me > 0)
        def _():
            halo(sweep, chunk).wait_recv()

    def slot_copy(sweep, k, peer, sender):
        return pltpu.make_async_remote_copy(
            src_ref=outgoing.at[sweep, peer],
            dst_ref=received.at[sweep, sender],
            send_sem=slot_send.at[sweep, k],
            recv_sem=slot_recv.at[sweep, k],
            device_id={"clus": peer},
        )

    def make_coeffs(sweep, low, high):
        source = columns if sweep == 0 else image

        @pl.loop(low, high)
        def _(c):
            v = source[c]
            basis = basis_in[c]
            by_real = jnp.dot(v, basis[0], preferred_element_type=F32)
            by_imag = jnp.dot(v, basis[1], preferred_element_type=F32)
            real = by_real[:rhs] - by_imag[rhs:]
            imag = by_imag[:rhs] + by_real[rhs:]
            coeffs[sweep, c] = jnp.concatenate([real, imag], -1).astype(BF16)

    def send_slots(sweep):
        @pl.loop(1, n)
        def _(k):
            peer = lax.rem(me + k, n)
            for j in range(slots):
                outgoing[sweep, peer, j] = coeffs[sweep, pairs[((me * n + peer) * slots + j) * 2]]
            slot_copy(sweep, k, peer, me).start()

        for j in range(slots):
            received[sweep, me, j] = coeffs[sweep, pairs[((me * n + me) * slots + j) * 2]]

    def near_phase(sweep, pieces, low, high, start, finish=None):
        @pl.loop(low, high)
        def _(c):
            product = None
            for buffers_of, base, count in pieces:
                buffer = buffers_of[sweep]
                for j in range(start, near_per, 2):
                    group = range(j, min(j + 2, near_per))
                    left, right = [], []
                    for slot in group:
                        at = c + off[c * near_per + slot] - base
                        at = jnp.where((at >= 0) & (at < count), at, count)
                        left.append(buffer[at])
                        right.append(jnp.concatenate([near[c, slot, 0], near[c, slot, 1]], -1))
                    left = left[0] if len(left) == 1 else jnp.concatenate(left, -1)
                    right = right[0] if len(right) == 1 else jnp.concatenate(right, 0)
                    term = jnp.dot(left, right, preferred_element_type=F32)
                    product = term if product is None else product + term
            real, imag = complex_rows(product)
            if start == 0:
                total[c, :rhs] = real
                total[c, rhs:] = imag
                return
            real = total[c, :rhs] + real
            imag = total[c, rhs:] + imag
            if finish is None:
                total[c, :rhs] = real
                total[c, rhs:] = imag
                return
            for target in finish:
                target[c, :rhs] = real.astype(BF16)
                target[c, rhs:] = imag.astype(BF16)

    def far(sweep):
        @pl.loop(1, n)
        def _(k):
            sender = lax.rem(me + n - k, n)
            slot_copy(sweep, k, lax.rem(me + k, n), sender).wait_recv()

        @pl.loop(0, n)
        def _(e):
            for j in range(slots):
                weighted[e, j] = jnp.dot(received[sweep, e, j], square[e, j], preferred_element_type=F32)

        @pl.loop(0, clusters)
        def _(c):
            def add(e, value):
                for j in range(slots):
                    hit = (pairs[((e * n + me) * slots + j) * 2 + 1] == c).astype(F32)
                    value = value + weighted[e, j] * hit
                return value

            gathered = lax.fori_loop(0, n, add, jnp.zeros((rhs, 2 * width), F32)).astype(BF16)
            real, imag = basis_out[c, 0], basis_out[c, 1]
            upper = jnp.concatenate([real, imag], -1)
            lower = jnp.concatenate([-imag, real], -1)
            term = jnp.dot(gathered, jnp.concatenate([upper, lower], 0), preferred_element_type=F32)
            total[c, :rhs] = total[c, :rhs] + term[:, :leaf]
            total[c, rhs:] = total[c, rhs:] + term[:, leaf:]

    send_halo(0, HI_A)
    send_halo(0, LO_A)
    make_coeffs(0, 0, clusters)
    send_slots(0)
    send_halo(0, HI_B)
    send_halo(0, LO_B)

    own_0[:clusters] = columns[...]

    @pl.loop(0, n)
    def _(e):
        for j in range(slots):
            bound = rank[(e * n + me) * slots + j]
            real, imag = coupling[e, j, 0], coupling[e, j, 1]
            full = jnp.concatenate(
                [jnp.concatenate([real, imag], -1), jnp.concatenate([-imag, real], -1)], 0
            )
            here = lax.broadcasted_iota(jnp.int32, full.shape, 0) % width
            there = lax.broadcasted_iota(jnp.int32, full.shape, 1) % width
            keep = (here < bound) & (there < bound)
            square[e, j] = jnp.where(keep, full.astype(F32), 0.0).astype(BF16)

    fetch().wait()
    own_piece = (own, 0, clusters)
    hi_a_piece = ((hi_a_0, hi_a_1), clusters, half)
    hi_b_piece = ((hi_b_0, hi_b_1), clusters + half, half)
    lo_a_piece = ((lo_a_0, lo_a_1), -half, half)
    lo_b_piece = ((lo_b_0, lo_b_1), -clusters, half)

    near_phase(0, (own_piece,), 0, clusters, 0)
    wait_halo(0, HI_A)
    near_phase(0, (hi_a_piece,), 0, clusters, 1)
    wait_halo(0, LO_A)
    near_phase(0, (lo_a_piece,), 0, clusters, 1)
    far(0)
    wait_halo(0, HI_B)
    near_phase(0, (hi_b_piece,), half, clusters, 1, (image, first))
    send_halo(1, HI_B)
    send_halo(1, LO_A)
    make_coeffs(1, half, clusters)
    wait_halo(0, LO_B)
    near_phase(0, (lo_b_piece,), 0, half, 1, (image, first))

    send_halo(1, HI_A)
    make_coeffs(1, 0, half)
    send_slots(1)
    send_halo(1, LO_B)
    own_1[:clusters] = image[...]
    near_phase(1, (own_piece,), 0, clusters, 0)
    wait_halo(1, LO_A)
    near_phase(1, (lo_a_piece,), 0, clusters, 1)
    wait_halo(1, HI_B)
    near_phase(1, (hi_b_piece,), half, clusters, 1)
    far(1)
    wait_halo(1, HI_A)
    near_phase(1, (hi_a_piece,), half, clusters, 1, (second,))
    near_phase(1, (hi_a_piece,), 0, half, 1)
    wait_halo(1, LO_B)
    near_phase(1, (lo_b_piece,), 0, half, 1, (second,))

    for sweep in range(2):
        for chunk in range(4):
            halo_sent(sweep, chunk)

        @pl.loop(1, n)
        def _(k):
            slot_copy(sweep, k, lax.rem(me + k, n), me).wait_send()


def on_device(n, input_columns, near_blocks, near_off, basis_in, coupling, basis_out, far_pairs, far_rank):
    clusters, parts, rhs, leaf = input_columns.shape
    near_per = near_blocks.shape[1]
    slots, width = coupling.shape[2], coupling.shape[4]
    rows = parts * rhs
    half = clusters // 2
    vmem = pl.BlockSpec(memory_space=pltpu.VMEM)
    smem = pl.BlockSpec(memory_space=pltpu.SMEM)
    shape = jax.ShapeDtypeStruct((clusters, rows, leaf), BF16)
    halo = pltpu.VMEM((half + 1, rows, leaf), BF16)
    first, second = pl.pallas_call(
        functools.partial(kernel, n),
        out_shape=(shape, shape),
        in_specs=[smem, smem, smem, vmem, pl.BlockSpec(memory_space=pl.ANY), vmem, vmem, vmem],
        out_specs=(vmem, vmem),
        scratch_shapes=[
            pltpu.VMEM(near_blocks.shape, BF16),
            pltpu.VMEM((clusters + 1, rows, leaf), BF16),
            pltpu.VMEM((clusters + 1, rows, leaf), BF16),
            pltpu.VMEM((clusters, rows, leaf), BF16),
            halo, halo, halo, halo,
            halo, halo, halo, halo,
            pltpu.VMEM((clusters, rows, leaf), F32),
            pltpu.VMEM((2, clusters, rhs, 2 * width), BF16),
            pltpu.VMEM((2, n, slots, rhs, 2 * width), BF16),
            pltpu.VMEM((2, n, slots, rhs, 2 * width), BF16),
            pltpu.VMEM((n, slots, 2 * width, 2 * width), BF16),
            pltpu.VMEM((n, slots, rhs, 2 * width), F32),
            pltpu.SemaphoreType.DMA,
            pltpu.SemaphoreType.DMA((2, 4)),
            pltpu.SemaphoreType.DMA((2, 4)),
            pltpu.SemaphoreType.DMA((2, n)),
            pltpu.SemaphoreType.DMA((2, n)),
        ],
        compiler_params=pltpu.CompilerParams(
            collective_id=0, has_side_effects=True, vmem_limit_bytes=60 * 1024 * 1024
        ),
        name="sweeps",
    )(
        near_off.reshape(-1),
        far_pairs.reshape(-1),
        far_rank.reshape(-1),
        input_columns.reshape(clusters, rows, leaf),
        near_blocks,
        basis_in,
        coupling[0],
        basis_out,
    )
    return first.reshape(input_columns.shape), second.reshape(input_columns.shape)


def solution(mesh):
    in_specs = (
        P(("freq", "clus"), None, "rhs", None),
        P(("freq", "clus"), None, None, None, None),
        P("clus", None),
        P(("freq", "clus"), None, None, None),
        P(("freq", "clus"), None, None, None, None, None),
        P(("freq", "clus"), None, None, None),
        P(),
        P(),
    )
    out_specs = (P(("freq", "clus"), None, "rhs", None), P(("freq", "clus"), None, "rhs", None))
    return jax.shard_map(
        functools.partial(on_device, mesh.shape["clus"]),
        mesh=mesh,
        in_specs=in_specs,
        out_specs=out_specs,
        check_vma=False,
    )
```

time: 94.9 us -> 88.7 us (0.935); the launches traced: 94.2 us -> 86.9 us
  Pallas kernels: 0 us -> 75.5 us
  waiting for transfers between devices: 28.5 us -> 0 us
  starting transfers between devices: 25 us -> 0 us
  matrix products: 17.7 us -> 0 us
  local copies, waits for them, and re-layouts: 17.9 us -> 10.8 us
  other arithmetic: 4 us -> 0 us
    pallas_call x0 -> x1, Pallas kernels: none -> 75.5 us  [on_device(): pl.pallas_call(functools.partial(kernel, n), out_shape=(shape, shape), in...]
    ppermute x4 -> x0, waiting for transfers between devices: 28.5 us -> none  [the longest x2 24.7 us: padded_2(): lax.ppermute(lax.slice_in_dim(block, block.shape[dim] - width, None, axis...]
    dot_general x10 -> x0, matrix products: 17.7 us -> none  [the longest x2 11.5 us: transposed_apply(): jnp.einsum('cjprt,cjqts->cpqrs', gathered, near_blocks, preferred_element...]
    ppermute x4 -> x0, starting transfers between devices: 13.5 us -> none  [the longest x2 6.92 us: padded_2(): lax.ppermute(lax.slice_in_dim(block, 0, width, axis=dim), axis, backward)]
    all_to_all x2 -> x0, starting transfers between devices: 11.5 us -> none  [transposed_apply(): lax.all_to_all(outgoing, 'clus', split_axis=0, concat_axis=0, tiled=True)]
    gather x4 -> x0, local copies, waits for them, and re-layouts: 8.54 us -> none  [the longest x2 5.71 us: transposed_apply(): gathered = padded[row_index]]
    unnamed x37 -> x6, local copies, waits for them, and re-layouts: 5.26 us -> 8.75 us
    concatenate x2 -> x0, other arithmetic: 2.9 us -> none  [padded_2(): block = jnp.concatenate([low, block, high], axis=dim)]
  transfers between devices with their start and end apart: 6 -> 0, of which waited for: 4 -> 0; matrix products, arithmetic and copies ran while one was open for 32% -> 0% of each run, Pallas kernels for 0% -> 0%
where the time goes in v1:
time: 88.7 us; the launch traced here: 86.9 us
  Pallas kernels  75.5 us (85%)
  local copies, waits for them, and re-layouts  10.8 us (12%)
    pallas_call x1, Pallas kernels, on_device(): pl.pallas_call(functools.partial(kernel, n), out_shape=(shape, shape), in...  75.5 us
    unnamed x6, local copies, waits for them, and re-layouts  8.75 us

profile of v1, /device:TPU:8, one launch (start us, length us, event | category | flops | bytes accessed | tf_op | source)
XLA Modules:
  0.0 86.9 jit_solution(9627993718654607913)
XLA Ops:
  0.6 0.8 copy.12
  1.4 0.6 reshape.22.off
  2.0 0.8 copy.14
  2.9 0.7 reshape.24.rank
  3.5 1.0 %copy.13 = s32[8,8,4,2]{3,2,1,0:T(4,128)S(1)} copy(s32[8,8,4,2]{1,3,2,0:T(2,128)} %param.14) | data formatting | bytes 4096 | tf_op args[6]
  4.5 0.7 reshape.23.pairs
  5.3 2.4 %copy.15.basis_in = bf16[16,2,128,64]{3,2,1,0:T(8,128)(2,1)} copy(bf16[16,2,128,64]{2,3,1,0:T(8,128)(2,1)} %param.11) | data formatting | bytes 1048576 | tf_op args[3]
  7.7 75.5 %sweeps.1 = (bf16[16,128,128]{2,1,0:T(8,128)(2,1)}, bf16[16,128,128]{2,1,0:T(8,128)(2,1)}) custom-call(s32[112]{0:T(128)} %reshape.22.off, s32[512]{0:T(512)} %reshape.23.pairs, s32[256]{0:T(256)} %reshape.24.rank, bf16[16,128,128]{2,1,0:T(8,128)(2,1)} %bitcast.5, bf16[16,7,2,128,128]{4,3,2,1,0:T(8,128)(2,1)} %near_hbm.1, ...), custom_call_target="tpu_custom_call" | custom-call | tf_op jit(solution)/shard_map/sweeps/pallas_call | solution.py:270
  83.2 1.9 %copy.18 = bf16[16,2,64,128]{3,2,1,0:T(8,128)(2,1)} copy(bf16[16,2,64,128]{3,2,1,0:T(8,128)(2,1)} %bitcast.7) | data formatting | bytes 1048576
  85.1 1.9 %copy.19 = bf16[16,2,64,128]{3,2,1,0:T(8,128)(2,1)} copy(bf16[16,2,64,128]{3,2,1,0:T(8,128)(2,1)} %bitcast.6) | data formatting | bytes 1048576

commit v2 on v1

v2 whole, which is shorter than its diff:
```python
import functools

import jax
import jax.numpy as jnp
from jax import lax
from jax.experimental import pallas as pl
from jax.experimental.pallas import tpu as pltpu
from jax.sharding import PartitionSpec as P

F32 = jnp.float32
BF16 = jnp.bfloat16

HI_A, HI_B, LO_A, LO_B = range(4)


def complex_rows(product):
    half_rows, half_cols = product.shape[0] // 2, product.shape[1] // 2
    real = product[:half_rows, :half_cols] - product[half_rows:, half_cols:]
    imag = product[:half_rows, half_cols:] + product[half_rows:, :half_cols]
    return real, imag


def kernel(
    n, off, pairs, rank, columns, near_hbm, basis_in_hbm, coupling_hbm, basis_out_hbm,
    first, second,
    near, basis_in, coupling, basis_out, own_0, own_1, hi_a_0, hi_b_0, lo_a_0, lo_b_0, hi_a_1, hi_b_1, lo_a_1, lo_b_1,
    total, coeffs, outgoing, received, square, weighted,
    fetch_sem, halo_send, halo_recv, slot_send, slot_recv,
):
    me = lax.axis_index("clus")
    clusters, rows, leaf = columns.shape
    half = clusters // 2
    slots = coupling.shape[1]
    width = coupling.shape[3]
    near_per = near.shape[1]
    rhs = rows // 2
    own = (own_0, own_1)
    buffers = ((hi_a_0, hi_b_0, lo_a_0, lo_b_0), (hi_a_1, hi_b_1, lo_a_1, lo_b_1))
    fetches = (
        (columns, own_0.at[pl.ds(0, clusters)]),
        (basis_in_hbm, basis_in),
        (near_hbm, near),
        (coupling_hbm, coupling),
        (basis_out_hbm, basis_out),
    )

    def fetch(i):
        return pltpu.make_async_copy(*fetches[i], fetch_sem.at[i])

    barrier = pltpu.get_barrier_semaphore()

    @pl.loop(1, n)
    def _(k):
        pl.semaphore_signal(barrier, inc=1, device_id={"clus": lax.rem(me + k, n)})

    for i in range(len(fetches)):
        fetch(i).start()
    pl.semaphore_wait(barrier, n - 1)

    starts = (0, half, half, 0)

    def halo(sweep, chunk):
        to_left = chunk in (HI_A, HI_B)
        source = columns if sweep == 0 else own_1
        peer = lax.rem(me + (n - 1 if to_left else 1), n)
        return pltpu.make_async_remote_copy(
            src_ref=source.at[pl.ds(starts[chunk], half)],
            dst_ref=buffers[sweep][chunk].at[pl.ds(0, half)],
            send_sem=halo_send.at[sweep, chunk],
            recv_sem=halo_recv.at[sweep, chunk],
            device_id={"clus": peer},
        )

    def send_halo(sweep, chunk):
        @pl.when(me > 0 if chunk in (HI_A, HI_B) else me < n - 1)
        def _():
            halo(sweep, chunk).start()

    def halo_sent(sweep, chunk):
        @pl.when(me > 0 if chunk in (HI_A, HI_B) else me < n - 1)
        def _():
            halo(sweep, chunk).wait_send()

    def wait_halo(sweep, chunk):
        @pl.when(me < n - 1 if chunk in (HI_A, HI_B) else me > 0)
        def _():
            halo(sweep, chunk).wait_recv()

    def slot_copy(sweep, k, peer, sender):
        return pltpu.make_async_remote_copy(
            src_ref=outgoing.at[sweep, peer],
            dst_ref=received.at[sweep, sender],
            send_sem=slot_send.at[sweep, k],
            recv_sem=slot_recv.at[sweep, k],
            device_id={"clus": peer},
        )

    def make_coeffs(sweep, low, high):
        @pl.loop(low, high, unroll=4)
        def _(c):
            v = own[sweep][c]
            basis = basis_in[c].reshape(2 * width, leaf)
            product = lax.dot_general(v, basis, (((1,), (1,)), ((), ())), preferred_element_type=F32)
            real, imag = complex_rows(product)
            coeffs[sweep, c] = jnp.concatenate([real, imag], -1).astype(BF16)

    def send_slots(sweep):
        @pl.loop(1, n)
        def _(k):
            peer = lax.rem(me + k, n)
            for j in range(slots):
                outgoing[sweep, peer, j] = coeffs[sweep, pairs[me, j, 0, peer]]
            slot_copy(sweep, k, peer, me).start()

        for j in range(slots):
            received[sweep, me, j] = coeffs[sweep, pairs[me, j, 0, me]]

    def store(targets, c, real, imag):
        for target in targets:
            target[c, :rhs] = real.astype(target.dtype)
            target[c, rhs:] = imag.astype(target.dtype)

    def near_phase(sweep, piece, low, high, start, finish=None):
        buffers_of, base, count = piece
        buffer = buffers_of[sweep]

        @pl.loop(low, high, unroll=2)
        def _(c):
            product = None
            for j in range(start, near_per, 2):
                left, right = [], []
                for slot in range(j, min(j + 2, near_per)):
                    at = c + off[slot, c] - base
                    at = jnp.where((at >= 0) & (at < count), at, count)
                    left.append(buffer[at])
                    right.append(jnp.concatenate([near[c, slot, 0], near[c, slot, 1]], -1))
                left = left[0] if len(left) == 1 else jnp.concatenate(left, -1)
                right = right[0] if len(right) == 1 else jnp.concatenate(right, 0)
                term = jnp.dot(left, right, preferred_element_type=F32)
                product = term if product is None else product + term
            real, imag = complex_rows(product)
            if start > 0:
                real = total[c, :rhs] + real
                imag = total[c, rhs:] + imag
            store((total,) if finish is None else finish, c, real, imag)

    def far(sweep, finish=None):
        @pl.loop(1, n)
        def _(k):
            sender = lax.rem(me + n - k, n)
            slot_copy(sweep, k, lax.rem(me + k, n), sender).wait_recv()

        @pl.loop(0, n, unroll=2)
        def _(e):
            for j in range(slots):
                weighted[e, j] = jnp.dot(received[sweep, e, j], square[e, j], preferred_element_type=F32)

        def add_far(low, high, targets):
            @pl.loop(low, high, unroll=2)
            def _(c):
                def add(e, value):
                    for j in range(slots):
                        hit = jnp.where(pairs[e, j, 1, me] == c, 1.0, 0.0)
                        value = value + weighted[e, j] * hit
                    return value

                gathered = lax.fori_loop(0, n, add, jnp.zeros((rhs, 2 * width), F32), unroll=4).astype(BF16)
                real, imag = basis_out[c, 0], basis_out[c, 1]
                upper = jnp.concatenate([real, imag], -1)
                lower = jnp.concatenate([-imag, real], -1)
                term = jnp.dot(gathered, jnp.concatenate([upper, lower], 0), preferred_element_type=F32)
                store(targets, c, total[c, :rhs] + term[:, :leaf], total[c, rhs:] + term[:, leaf:])

        add_far(half, clusters, (total,) if finish is None else finish)
        add_far(0, half, (total,))

    send_halo(0, HI_A)
    send_halo(0, LO_A)
    fetch(0).wait()
    fetch(1).wait()
    make_coeffs(0, 0, clusters)
    send_slots(0)
    send_halo(0, HI_B)
    send_halo(0, LO_B)

    zero = jnp.zeros((rows, leaf), BF16)
    for sweep in range(2):
        own[sweep][clusters] = zero
        for buffer in buffers[sweep]:
            buffer[half] = zero

    @pl.when(me == 0)
    def _():
        for sweep in range(2):
            for chunk in (LO_A, LO_B):
                buffers[sweep][chunk][...] = jnp.zeros_like(buffers[sweep][chunk])

    @pl.when(me == n - 1)
    def _():
        for sweep in range(2):
            for chunk in (HI_A, HI_B):
                buffers[sweep][chunk][...] = jnp.zeros_like(buffers[sweep][chunk])

    own_piece = (own, 0, clusters)
    hi_a_piece = ((hi_a_0, hi_a_1), clusters, half)
    hi_b_piece = ((hi_b_0, hi_b_1), clusters + half, half)
    lo_a_piece = ((lo_a_0, lo_a_1), -half, half)
    lo_b_piece = ((lo_b_0, lo_b_1), -clusters, half)

    fetch(2).wait()
    near_phase(0, own_piece, 0, clusters, 0)

    fetch(3).wait()
    fetch(4).wait()

    @pl.loop(0, n)
    def _(e):
        here = lax.broadcasted_iota(jnp.int32, (2 * width, 2 * width), 0) % width
        there = lax.broadcasted_iota(jnp.int32, (2 * width, 2 * width), 1) % width
        position = jnp.maximum(here, there)
        for j in range(slots):
            real, imag = coupling[e, j, 0], coupling[e, j, 1]
            full = jnp.concatenate(
                [jnp.concatenate([real, imag], -1), jnp.concatenate([-imag, real], -1)], 0
            )
            square[e, j] = jnp.where(position < rank[e, j, me], full.astype(F32), 0.0).astype(BF16)

    wait_halo(0, HI_A)
    near_phase(0, hi_a_piece, 0, clusters, 1)
    wait_halo(0, LO_A)
    near_phase(0, lo_a_piece, 0, clusters, 1)
    far(0)
    wait_halo(0, HI_B)
    near_phase(0, hi_b_piece, half, clusters, 1, (own_1, first))
    send_halo(1, HI_B)
    send_halo(1, LO_A)
    make_coeffs(1, half, clusters)
    wait_halo(0, LO_B)
    near_phase(0, lo_b_piece, 0, half, 1, (own_1, first))

    send_halo(1, HI_A)
    make_coeffs(1, 0, half)
    send_slots(1)
    send_halo(1, LO_B)
    near_phase(1, own_piece, 0, clusters, 0)
    wait_halo(1, HI_B)
    near_phase(1, hi_b_piece, half, clusters, 1)
    wait_halo(1, LO_A)
    near_phase(1, lo_a_piece, 0, clusters, 1)
    wait_halo(1, HI_A)
    near_phase(1, hi_a_piece, 0, clusters, 1)
    far(1, (second,))
    wait_halo(1, LO_B)
    near_phase(1, lo_b_piece, 0, half, 1, (second,))

    for sweep in range(2):
        for chunk in range(4):
            halo_sent(sweep, chunk)

        @pl.loop(1, n)
        def _(k):
            slot_copy(sweep, k, lax.rem(me + k, n), me).wait_send()


def on_device(n, input_columns, near_blocks, near_off, basis_in, coupling, basis_out, far_pairs, far_rank):
    clusters, parts, rhs, leaf = input_columns.shape
    near_per = near_blocks.shape[1]
    slots, width = coupling.shape[2], coupling.shape[4]
    rows = parts * rhs
    half = clusters // 2
    vmem = pl.BlockSpec(memory_space=pltpu.VMEM)
    smem = pl.BlockSpec(memory_space=pltpu.SMEM)
    hbm = pl.BlockSpec(memory_space=pltpu.HBM)
    basis_in = jnp.swapaxes(basis_in, 2, 3)
    shape = jax.ShapeDtypeStruct((clusters, rows, leaf), BF16)
    halo = pltpu.VMEM((half + 1, rows, leaf), BF16)
    first, second = pl.pallas_call(
        functools.partial(kernel, n),
        out_shape=(shape, shape),
        in_specs=[smem] * 3 + [hbm] * 5,
        out_specs=(vmem, vmem),
        scratch_shapes=[
            pltpu.VMEM(near_blocks.shape, BF16),
            pltpu.VMEM(basis_in.shape, BF16),
            pltpu.VMEM(coupling.shape[1:], BF16),
            pltpu.VMEM(basis_out.shape, BF16),
            pltpu.VMEM((clusters + 1, rows, leaf), BF16),
            pltpu.VMEM((clusters + 1, rows, leaf), BF16),
            halo, halo, halo, halo,
            halo, halo, halo, halo,
            pltpu.VMEM((clusters, rows, leaf), F32),
            pltpu.VMEM((2, clusters, rhs, 2 * width), BF16),
            pltpu.VMEM((2, n, slots, rhs, 2 * width), BF16),
            pltpu.VMEM((2, n, slots, rhs, 2 * width), BF16),
            pltpu.VMEM((n, slots, 2 * width, 2 * width), BF16),
            pltpu.VMEM((n, slots, rhs, 2 * width), F32),
            pltpu.SemaphoreType.DMA((5,)),
            pltpu.SemaphoreType.DMA((2, 4)),
            pltpu.SemaphoreType.DMA((2, 4)),
            pltpu.SemaphoreType.DMA((2, n)),
            pltpu.SemaphoreType.DMA((2, n)),
        ],
        compiler_params=pltpu.CompilerParams(
            collective_id=0, has_side_effects=True, vmem_limit_bytes=57 * 2**20
        ),
        name="sweeps",
    )(
        near_off.T,
        jnp.transpose(far_pairs, (0, 2, 3, 1)),
        jnp.swapaxes(far_rank, 1, 2),
        input_columns.reshape(clusters, rows, leaf),
        near_blocks,
        basis_in,
        coupling[0],
        basis_out,
    )
    return first.reshape(input_columns.shape), second.reshape(input_columns.shape)


def solution(mesh):
    in_specs = (
        P(("freq", "clus"), None, "rhs", None),
        P(("freq", "clus"), None, None, None, None),
        P("clus", None),
        P(("freq", "clus"), None, None, None),
        P(("freq", "clus"), None, None, None, None, None),
        P(("freq", "clus"), None, None, None),
        P(),
        P(),
    )
    out_specs = (P(("freq", "clus"), None, "rhs", None), P(("freq", "clus"), None, "rhs", None))
    return jax.shard_map(
        functools.partial(on_device, mesh.shape["clus"]),
        mesh=mesh,
        in_specs=in_specs,
        out_specs=out_specs,
        check_vma=False,
    )
```

time: 88.7 us -> 78.1 us (0.88)
  local copies, waits for them, and re-layouts: 10.8 us -> 3.76 us
  Pallas kernels: 75.5 us -> 72.3 us
    unnamed x6 -> x2, local copies, waits for them, and re-layouts: 8.75 us -> 3.76 us
    pallas_call x1, Pallas kernels: 75.5 us -> 72.3 us  [on_device(): pl.pallas_call(functools.partial(kernel, n), out_shape=(shape, shape), in...]
    reshape x3 -> x0, local copies, waits for them, and re-layouts: 2.04 us -> none  [the longest x1 0.74 us: on_device(): far_pairs.reshape(-1)]
where the time goes in v2:
time: 78.1 us; the launch traced here: 76.7 us
  Pallas kernels  72.3 us (93%)
  local copies, waits for them, and re-layouts  3.76 us (5%)
    pallas_call x1, Pallas kernels, on_device(): pl.pallas_call(functools.partial(kernel, n), out_shape=(shape, shape), in...  72.3 us
    unnamed x2, local copies, waits for them, and re-layouts  3.76 us

profile of v2, /device:TPU:8, one launch (start us, length us, event | category | flops | bytes accessed | tf_op | source)
XLA Modules:
  0.0 76.7 jit_solution(8248136265194567880)
XLA Ops:
  0.6 72.3 %sweeps.1 = (bf16[16,128,128]{2,1,0:T(8,128)(2,1)}, bf16[16,128,128]{2,1,0:T(8,128)(2,1)}) custom-call(s32[7,16]{1,0:T(8,128)} %bitcast.15, s32[8,4,2,8]{3,2,1,0:T(2,128)} %bitcast.13, s32[8,4,8]{2,1,0:T(4,128)} %bitcast.14, bf16[16,128,128]{2,1,0:T(8,128)(2,1)} %bitcast.9, bf16[16,7,2,128,128]{4,3,2,1,0:T(8,128)(2,1)} %near_hbm.1, ...), custom_call_target="tpu_custom_call" | custom-call | tf_op jit(solution)/shard_map/sweeps/pallas_call | solution.py:277
  73.0 1.9 %copy.12 = bf16[16,2,64,128]{3,2,1,0:T(8,128)(2,1)} copy(bf16[16,2,64,128]{3,2,1,0:T(8,128)(2,1)} %bitcast.12) | data formatting | bytes 1048576
  74.8 1.9 %copy.13 = bf16[16,2,64,128]{3,2,1,0:T(8,128)(2,1)} copy(bf16[16,2,64,128]{3,2,1,0:T(8,128)(2,1)} %bitcast.11) | data formatting | bytes 1048576

commit v3 on v2

--- a/solution.py
+++ b/solution.py
@@ -104,15 +104,15 @@
             real, imag = complex_rows(product)
             coeffs[sweep, c] = jnp.concatenate([real, imag], -1).astype(BF16)
 
-    def send_slots(sweep):
-        @pl.loop(1, n)
+    def send_slots(sweep, part, of):
+        @pl.loop(1 + (n - 1) * part // of, 1 + (n - 1) * (part + 1) // of)
         def _(k):
             peer = lax.rem(me + k, n)
             for j in range(slots):
                 outgoing[sweep, peer, j] = coeffs[sweep, pairs[me, j, 0, peer]]
             slot_copy(sweep, k, peer, me).start()
 
-        for j in range(slots):
+        for j in range(slots if part == 0 else 0):
             received[sweep, me, j] = coeffs[sweep, pairs[me, j, 0, me]]
 
     def store(targets, c, real, imag):
@@ -174,12 +174,12 @@
         add_far(half, clusters, (total,) if finish is None else finish)
         add_far(0, half, (total,))
 
-    send_halo(0, HI_A)
-    send_halo(0, LO_A)
     fetch(0).wait()
     fetch(1).wait()
     make_coeffs(0, 0, clusters)
-    send_slots(0)
+    send_slots(0, 0, 1)
+    send_halo(0, HI_A)
+    send_halo(0, LO_A)
     send_halo(0, HI_B)
     send_halo(0, LO_B)
 
@@ -238,9 +238,9 @@
     wait_halo(0, LO_B)
     near_phase(0, lo_b_piece, 0, half, 1, (own_1, first))
 
+    make_coeffs(1, 0, half)
+    send_slots(1, 0, 1)
     send_halo(1, HI_A)
-    make_coeffs(1, 0, half)
-    send_slots(1)
     send_halo(1, LO_B)
     near_phase(1, own_piece, 0, clusters, 0)
     wait_halo(1, HI_B)
@@ -301,7 +301,7 @@
             pltpu.SemaphoreType.DMA((2, n)),
         ],
         compiler_params=pltpu.CompilerParams(
-            collective_id=0, has_side_effects=True, vmem_limit_bytes=57 * 2**20
+            collective_id=0, has_side_effects=True, vmem_limit_bytes=52 * 2**20
         ),
         name="sweeps",
     )(

time: 78.1 us -> 77.8 us (level); the launches traced: 76.7 us -> 77.5 us
  local copies, waits for them, and re-layouts: 3.76 us -> 4.78 us
    unnamed x2 -> x10, local copies, waits for them, and re-layouts: 3.76 us -> 4.78 us
where the time goes in v3:
time: 77.8 us; the launch traced here: 77.5 us
  Pallas kernels  72.1 us (93%)
  local copies, waits for them, and re-layouts  4.78 us (6%)
    pallas_call x1, Pallas kernels, on_device(): pl.pallas_call(functools.partial(kernel, n), out_shape=(shape, shape), in...  72.1 us
    unnamed x10, local copies, waits for them, and re-layouts  4.78 us

profile of v3, /device:TPU:8, one launch (start us, length us, event | category | flops | bytes accessed | tf_op | source)
XLA Modules:
  0.0 77.5 jit_solution(3043836111699179973)
XLA Ops:
  0.6 0.0 copy-start
  0.6 1.0 %copy-done = bf16[16,2,64,128]{3,2,1,0:T(8,128)(2,1)S(1)} copy-done((bf16[16,2,64,128]{3,2,1,0:T(8,128)(2,1)S(1)}, bf16[16,2,64,128]{3,2,1,0:T(8,128)(2,1)}, u32[]{:S(2)}) %copy-start) | copy-done | bytes 524312
  1.7 0.0 copy-start.1
  1.7 0.8 copy-done.1
  2.4 0.0 copy-start.2
  2.4 0.7 copy-done.2
  3.2 0.0 copy-start.3
  3.2 0.7 copy-done.3
  3.8 72.1 %sweeps.1 = (bf16[16,128,128]{2,1,0:T(8,128)(2,1)S(1)}, bf16[16,128,128]{2,1,0:T(8,128)(2,1)S(1)}) custom-call(s32[7,16]{1,0:T(8,128)S(1)} %bitcast.13, s32[8,4,2,8]{3,2,1,0:T(2,128)S(1)} %bitcast.11, s32[8,4,8]{2,1,0:T(4,128)S(1)} %bitcast.12, bf16[16,128,128]{2,1,0:T(8,128)(2,1)S(1)} %bitcast.8, bf16[16,7,2,128,128]{4,3,2,1,0:T(8,128)(2,1)} %near_hbm.1, ...), custom_call_target="tpu_custom_call" | custom-call | tf_op jit(solution)/shard_map/sweeps/pallas_call | solution.py:277
  75.9 0.8 %copy.12 = bf16[16,2,64,128]{3,2,1,0:T(8,128)(2,1)} copy(bf16[16,2,64,128]{3,2,1,0:T(8,128)(2,1)S(1)} %bitcast.10) | data formatting | bytes 1048576
  76.7 0.8 %copy.13 = bf16[16,2,64,128]{3,2,1,0:T(8,128)(2,1)} copy(bf16[16,2,64,128]{3,2,1,0:T(8,128)(2,1)S(1)} %bitcast.9) | data formatting | bytes 1048576
Async XLA Ops:
  0.6 1.0 %copy-start = (bf16[16,2,64,128]{3,2,1,0:T(8,128)(2,1)S(1)}, bf16[16,2,64,128]{3,2,1,0:T(8,128)(2,1)}, u32[]{:S(2)}) copy-start(bf16[16,2,64,128]{3,2,1,0:T(8,128)(2,1)} %param.8) | copy-start | bytes 1572868
  1.7 0.8 copy-start.1
  2.4 0.7 copy-start.2
  3.2 0.7 copy-start.3
